TPU v7x, 256 devices: a whole 4x4x8 slice. The times are simulated.
256 devices in a mesh: ctx: 32 (over z, y_lo, core), head: 8 (over x, y_hi).
Axes of the slice: x: 4, y: 4 (y_hi: 2, y_lo: 2; y = y_hi * 2 + y_lo), z: 8, core: 2. Of those that a mesh axis runs over, the one named last changes fastest.
Arguments:
- query: bfloat16 [4096, 8192], P('ctx', 'head'), may hold values from -11 to 11
- key_in: bfloat16 [4096, 1024], P('ctx', 'head'), may hold values from -11 to 11
- value: bfloat16 [4096, 1024], P('ctx', 'head'), may hold values from -6 to 6
- grad_y: bfloat16 [4096, 8192], P('ctx', 'head'), may hold values from -6 to 6
- w_out: bfloat16 [8192, 8192], P('head', 'ctx'), may hold values from -0.0625 to 0.0625
- parent: int32 [32], replicated, may hold values from 1 to 31, as said below
Outputs:
- grad_query: bfloat16 [4096, 8192], P('ctx', 'head')
- grad_key: bfloat16 [4096, 1024], P('ctx', 'head')
- grad_value: bfloat16 [4096, 1024], P('ctx', 'head')
Inputs may be any that keep to these rules, and one draw needn't show every extreme that they name: The shared prefix is blocks 32 - 4 to 31: parent[31] = 31 and parent[b] = b + 1 for the other prefix blocks; the earlier blocks form particles of 4 consecutive blocks, in which each block's parent is the block after it, except a particle's last block, whose parent is a block of the shared prefix.
All inputs are finite; a program needn't handle non-finite values.
Results may differ from a plain program's by a relative error of at most 0.014.
Values may be sent and summed in bfloat16 or wider, within the bound.
A program may use at most 128 MiB of HBM per device.

v0:
```python
import jax
import jax.numpy as jnp
from jax import lax
from jax.sharding import PartitionSpec as P

HPG = 8
DH = 128
BLOCK = 128


def shifted(value, axis, steps):
    count = lax.axis_size(axis)
    pairs = [(source, (source + steps) % count) for source in range(count)]
    return lax.ppermute(value, axis, pairs)


def ancestors(parent):
    count = parent.shape[0]
    index = jnp.arange(count, dtype=jnp.int32)
    start = (index[:, None] == index[None, :]).astype(jnp.int32)

    def advance(step, state):
        current, marks = state
        current = jnp.sum(jnp.where(current[:, None] == index[None, :], parent[None, :], 0), axis=1)
        marks = jnp.maximum(marks, (current[:, None] == index[None, :]).astype(jnp.int32))
        return (current, marks)

    return lax.fori_loop(0, count, advance, (index, start))[1]


def per_device(query, key_in, value, grad_y, w_out, parent):
    tokens_here = query.shape[0]
    groups = key_in.shape[1] // DH
    scale = DH ** (-0.5)
    cycle_size = lax.axis_size("ctx")
    place = lax.axis_index("ctx")
    full_rows = lax.all_gather(grad_y, "head", axis=1, tiled=True)
    grad_attn = lax.dot_general(
        full_rows,
        lax.all_gather(w_out, "ctx", axis=1, tiled=True),
        (((1,), (1,)), ((), ())),
        preferred_element_type=jnp.float32,
    ).astype(jnp.bfloat16)
    visible = ancestors(parent)
    block_count = parent.shape[0]
    blocks_here = tokens_here // BLOCK
    local_visible = lax.dynamic_slice_in_dim(visible, place * blocks_here, blocks_here, 0).astype(
        jnp.float32
    )
    query_pos = place * tokens_here + jnp.arange(tokens_here, dtype=jnp.int32)
    query_block = query_pos // BLOCK
    owned = place * blocks_here + jnp.arange(blocks_here, dtype=jnp.int32)
    query_select = (query_block[:, None] == owned[None, :]).astype(jnp.float32)
    query_visible = jnp.dot(query_select, local_visible)
    block_index = jnp.arange(block_count, dtype=jnp.int32)

    def make_mask(start, count):
        key_pos = start + jnp.arange(count, dtype=jnp.int32)
        key_block = key_pos // BLOCK
        key_select = (key_block[:, None] == block_index[None, :]).astype(jnp.float32)
        allowed = jnp.dot(query_visible, key_select.T) > 0.5
        return allowed & (
            (query_block[:, None] != key_block[None, :]) | (key_pos[None, :] <= query_pos[:, None])
        )

    query_heads = query.reshape(tokens_here, groups, HPG, DH).transpose(1, 2, 0, 3)
    grad_heads = grad_attn.reshape(tokens_here, groups, HPG, DH).transpose(1, 2, 0, 3)

    def split_heads(matrix):
        return matrix.reshape(matrix.shape[0], groups, DH).transpose(1, 0, 2)

    def join_heads(tensor):
        return tensor.transpose(1, 0, 2).reshape(tensor.shape[1], groups * DH)

    stat_shape = (groups, HPG, tokens_here)
    key_piece = lax.all_gather(key_in, "ctx", axis=0, tiled=True)
    value_piece = lax.all_gather(value, "ctx", axis=0, tiled=True)
    mask = make_mask(jnp.int32(0), key_piece.shape[0])
    statistics_top = jnp.full(stat_shape, -1e30, jnp.float32)
    scores = (
        jnp.einsum(
            "ghqd,gkd->ghqk",
            query_heads,
            split_heads(key_piece),
            preferred_element_type=jnp.float32,
        )
        * scale
    )
    masked = jnp.where(mask, scores, -1e30)
    new_top = jnp.maximum(statistics_top, jnp.max(masked, axis=3))
    weights = jnp.where(mask, jnp.exp(scores - new_top[..., None]), 0.0)
    dprob = jnp.einsum(
        "ghqd,gkd->ghqk", grad_heads, split_heads(value_piece), preferred_element_type=jnp.float32
    )
    statistics_norm = jnp.sum(weights, axis=3)
    weighted = jnp.sum(weights * dprob, axis=3)
    top, norm, weighted = (new_top, statistics_norm, weighted)
    delta = weighted / norm

    def contribution(key_piece, value_piece, mask):
        key_heads = split_heads(key_piece)
        value_heads = split_heads(value_piece)
        scores = (
            jnp.einsum("ghqd,gkd->ghqk", query_heads, key_heads, preferred_element_type=jnp.float32)
            * scale
        )
        prob = jnp.where(mask, jnp.exp(scores - top[..., None]), 0.0) / norm[..., None]
        dprob = jnp.einsum(
            "ghqd,gkd->ghqk", grad_heads, value_heads, preferred_element_type=jnp.float32
        )
        value_part = jnp.einsum(
            "ghqk,ghqd->gkd",
            prob.astype(jnp.bfloat16),
            grad_heads,
            preferred_element_type=jnp.float32,
        )
        dscore = (prob * (dprob - delta[..., None])).astype(jnp.bfloat16)
        query_part = (
            jnp.einsum("ghqk,gkd->ghqd", dscore, key_heads, preferred_element_type=jnp.float32)
            * scale
        )
        key_part = (
            jnp.einsum("ghqk,ghqd->gkd", dscore, query_heads, preferred_element_type=jnp.float32)
            * scale
        )
        return (query_part, join_heads(key_part), join_heads(value_part))

    def visit(key_piece, value_piece, start):
        mask = make_mask(start, key_piece.shape[0])
        return contribution(key_piece, value_piece, mask)

    grad_query = jnp.zeros((groups, HPG, tokens_here, DH), jnp.float32)

    def turn_one(step, state):
        grad_q, key_piece, value_piece, key_sum, value_sum = state
        owner = (place - step) % cycle_size
        query_part, key_part, value_part = visit(key_piece, value_piece, owner * tokens_here)
        grad_q = grad_q + query_part
        key_sum = key_sum + key_part
        value_sum = value_sum + value_part
        key_piece, value_piece = shifted((key_piece, value_piece), "ctx", 1)
        key_sum, value_sum = shifted((key_sum, value_sum), "ctx", 1)
        return (grad_q, key_piece, value_piece, key_sum, value_sum)

    zero_rows = jnp.zeros((tokens_here, groups * DH), jnp.float32)
    state = (grad_query, key_in, value, zero_rows, zero_rows)
    grad_query, unused_key, unused_value, grad_key, grad_value = lax.fori_loop(
        0, cycle_size, turn_one, state
    )
    grad_query = (
        grad_query.transpose(2, 0, 1, 3)
        .reshape(tokens_here, groups * HPG * DH)
        .astype(jnp.bfloat16)
    )
    return (grad_query, grad_key.astype(jnp.bfloat16), grad_value.astype(jnp.bfloat16))


def solution(mesh):
    placed = (
        P("ctx", "head"),
        P("ctx", "head"),
        P("ctx", "head"),
        P("ctx", "head"),
        P("head", "ctx"),
        P(),
    )
    return jax.shard_map(
        per_device,
        mesh=mesh,
        in_specs=placed,
        out_specs=(P("ctx", "head"), P("ctx", "head"), P("ctx", "head")),
        check_vma=False,
    )
```

profile of v0, /device:TPU:2, one launch (start us, length us, event | category | flops | bytes accessed | tf_op | source)
XLA Modules:
  0.0 608.8 jit_solution(9453911751109003068)
XLA Ops:
  12.1 29.5 %while.40 = (s32[]{:T(128)}, s32[32]{0:T(128)S(1)}, s32[32,32]{1,0:T(8,128)S(1)}, s32[32]{0:T(128)}, s32[]{:T(128)}) while((s32[]{:T(128)}, s32[32]{0:T(128)S(1)}, s32[32,32]{1,0:T(8,128)S(1)}, s32[32]{0:T(128)}, s32[]{:T(128)}) %tuple.80), condition=%wide.region_2.3_spmd.clone.clone, body=%wide.region_0.2_spmd.clone.clone.sunk | while | flops 6114 | bytes 9021 | solution.py:28
  43.7 33.4 %all-gather.5.cloned.1.call-done = bf16[4096,128]{1,0:T(8,128)(2,1)} async-done(((bf16[128,128]{1,0:T(8,128)(2,1)}), bf16[4096,128]{1,0:T(8,128)(2,1)}) %all-gather.5.cloned.1.call-update) | async-done | bytes 1048592 | tf_op jit(solution)/shard_map/all_gather | solution.py:76
  77.2 4.5 select_reduce_fusion.1
  81.7 5.7 copy-done
  87.4 4.9 fusion.35
  92.3 47.1 %all-gather.7.cloned.1.call-done = bf16[128,8192]{1,0:T(8,128)(2,1)} async-done(((bf16[128,1024]{1,0:T(8,128)(2,1)}), bf16[128,8192]{1,0:T(8,128)(2,1)}) %all-gather.7.cloned.1.call-update) | async-done | bytes 2097168 | tf_op jit(solution)/shard_map/all_gather | solution.py:37
  139.3 123.7 %all-gather.9.cloned.1.call-done = bf16[1024,8192]{1,0:T(8,128)(2,1)} async-done(((bf16[1024,256]{1,0:T(8,128)(2,1)}), bf16[1024,8192]{1,0:T(8,128)(2,1)}) %all-gather.9.cloned.1.call-update) | async-done | bytes 16777232 | tf_op jit(solution)/shard_map/all_gather | solution.py:40
  263.0 12.1 %fusion.38 = bf16[16,8,8,128]{3,1,2,0:T(8,128)(2,1)S(1)} fusion(bf16[128,8192]{1,0:T(8,128)(2,1)} %all-gather.7.cloned.1.call-done, bf16[1024,8192]{1,0:T(8,128)(2,1)} %all-gather.9.cloned.1.call-done), kind=kOutput, calls=%fused_computation.60 | convolution fusion | flops 2147614720 | bytes 19136512 | tf_op jit(solution)/shard_map/dot_general | solution.py:38
  275.2 52.8 %all-gather.11.cloned.1.call-done = bf16[4096,128]{1,0:T(8,128)(2,1)} async-done(((bf16[128,128]{1,0:T(8,128)(2,1)}), bf16[4096,128]{1,0:T(8,128)(2,1)}) %all-gather.11.cloned.1.call-update) | async-done | bytes 1048592 | tf_op jit(solution)/shard_map/all_gather | solution.py:77
  328.1 9.0 %multiply_reduce_fusion = f32[8,128]{1,0:T(8,128)S(1)} fusion(f32[8,128,4096]{2,1,0:T(8,128)} %copy-done, f32[8,128]{1,0:T(8,128)S(1)} %get-tuple-element.648, pred[128,4096]{1,0:T(8,128)(4,1)S(1)} %fusion.36, bf16[4096,128]{1,0:T(8,128)(2,1)} %all-gather.11.cloned.1.call-done, bf16[128,1,8,128]{3,2,0,1:T(8,128)(2,1)S(1)} %bitcast.121), kind=kOutput, calls=%fused_computation.51 | convolution fusion | flops 1094712320 | bytes 18620416 | tf_op jit(solution)/shard_map/ghqd,gkd->ghqk/dot_general | solution.py:92
  337.1 263.0 %while.41 = (s32[]{:T(128)}, f32[1,8,128,128]{3,2,1,0:T(8,128)S(1)}, bf16[128,128]{1,0:T(8,128)(2,1)S(1)}, bf16[128,128]{1,0:T(8,128)(2,1)S(1)}, f32[128,128]{1,...) while((s32[]{:T(128)}, ...), condition=%wide.region_7.8_spmd.clone.clone.clone, body=%wide.region_6.7_spmd.clone.clone.clone.sunk | while | flops 170405904 | bytes 5817452 | solution.py:147
  343.2 2.5 collective-permute-done.2
  360.3 1.7 collective-permute-done.2
  364.7 1.8 collective-permute-start.3
  368.5 1.7 collective-permute-done.2
  373.7 2.6 collective-permute-done.1
  376.7 1.7 collective-permute-done.2
  381.8 2.7 collective-permute-done.1
  384.9 1.7 collective-permute-done.2
  390.5 2.2 collective-permute-done.1
  393.1 1.7 collective-permute-done.2
  397.4 2.5 collective-permute-start.3
  401.2 1.7 collective-permute-done.2
  405.8 2.2 collective-permute-start.3
  409.4 1.9 collective-permute-done.2
  414.0 2.2 collective-permute-start.3
  417.8 1.7 collective-permute-done.2
  422.2 2.2 collective-permute-start.3
  426.0 1.7 collective-permute-done.2
  430.4 2.2 collective-permute-start.3
  438.6 2.2 collective-permute-start.3
  442.3 1.7 collective-permute-done.2
  446.7 2.2 collective-permute-start.3
  454.9 2.2 collective-permute-start.3
  458.7 1.7 collective-permute-done.2
  463.1 2.2 collective-permute-start.3
  471.3 2.2 collective-permute-start.3
  475.0 1.7 collective-permute-done.2
  479.4 2.2 collective-permute-start.3
  483.2 1.7 collective-permute-done.2
  487.6 2.2 collective-permute-start.3
  491.4 1.7 collective-permute-done.2
  495.8 2.2 collective-permute-start.3
  499.6 1.7 collective-permute-done.2
  504.0 2.2 collective-permute-start.3
  507.7 1.7 collective-permute-done.2
  512.2 2.2 collective-permute-start.3
  520.3 2.2 collective-permute-start.3
  524.1 1.7 collective-permute-done.2
  528.5 2.2 collective-permute-start.3
  536.7 2.2 collective-permute-start.3
  540.4 1.7 collective-permute-done.2
  544.9 2.2 collective-permute-start.3
  553.0 2.2 collective-permute-start.3
  556.8 1.7 collective-permute-done.2
  561.2 2.2 collective-permute-start.3
  565.0 1.7 collective-permute-done.2
  569.4 2.2 collective-permute-start.3
  573.2 1.7 collective-permute-done.2
  577.6 2.2 collective-permute-start.3
  581.3 1.7 collective-permute-done.2
  585.7 2.2 collective-permute-start.3
  589.5 1.7 collective-permute-done.2
  593.9 2.2 collective-permute-start.3
  (687 shorter events, 192.7 us)
Async XLA Ops:
  7.2 70.0 %all-gather.5.cloned.1.call-start = ((), (), s32[]{:S(2)}) async-start(), calls=%async_computation | async-start | bytes 1081344 | tf_op jit(solution)/shard_map/all_gather | solution.py:76
  10.0 129.4 %all-gather.7.cloned.1.call-start = ((), (), s32[]{:S(2)}) async-start(), calls=%async_computation.1 | async-start | bytes 2359296 | tf_op jit(solution)/shard_map/all_gather | solution.py:37
  10.7 252.3 %all-gather.9.cloned.1.call-start = ((), (), s32[]{:S(2)}) async-start(), calls=%async_computation.2 | async-start | bytes 17301504 | tf_op jit(solution)/shard_map/all_gather | solution.py:40
  11.5 316.6 %all-gather.11.cloned.1.call-start = ((), (), s32[]{:S(2)}) async-start(), calls=%async_computation.3 | async-start | bytes 1081344 | tf_op jit(solution)/shard_map/all_gather | solution.py:77
  339.8 5.9 collective-permute-start.2
  340.4 6.0 collective-permute-start.3
  348.0 5.9 collective-permute-start.2
  348.3 6.2 %collective-permute-start.3 = (f32[128,128]{1,0:T(8,128)S(1)}, f32[128,128]{1,0:T(8,128)S(1)}, u32[]{:S(2)}, u32[]{:S(2)}) collective-permute-start(f32[128,128]{1,0:T(8,128)S(1)} %fusion.91), channel_id=1, source_target_pairs={{0,8},{8,16},{16,24},{24,32},{32,40},{40,48},{48,56},{56,64},{64,7... | collective-permute-start | bytes 196616 | tf_op jit(solution)/shard_map/while/body/eval_jaxpr/ppermute | solution.py:14
  356.1 5.9 collective-permute-start.2
  356.5 6.2 %collective-permute-start.3 = (f32[128,128]{1,0:T(8,128)S(1)}, f32[128,128]{1,0:T(8,128)S(1)}, u32[]{:S(2)}, u32[]{:S(2)}) collective-permute-start(f32[128,128]{1,0:T(8,128)S(1)} %fusion.91), channel_id=1, source_target_pairs={{0,8},{8,16},{16,24},{24,32},{32,40},{40,48},{48,56},{56,64},{64,7... | collective-permute-start | bytes 196616 | tf_op jit(solution)/shard_map/while/body/eval_jaxpr/ppermute | solution.py:14
  364.3 5.9 collective-permute-start.2
  364.7 6.2 %collective-permute-start.3 = (f32[128,128]{1,0:T(8,128)S(1)}, f32[128,128]{1,0:T(8,128)S(1)}, u32[]{:S(2)}, u32[]{:S(2)}) collective-permute-start(f32[128,128]{1,0:T(8,128)S(1)} %fusion.91), channel_id=1, source_target_pairs={{0,8},{8,16},{16,24},{24,32},{32,40},{40,48},{48,56},{56,64},{64,7... | collective-permute-start | bytes 196616 | tf_op jit(solution)/shard_map/while/body/eval_jaxpr/ppermute | solution.py:14
  372.5 5.9 collective-permute-start.2
  372.9 6.2 %collective-permute-start.3 = (f32[128,128]{1,0:T(8,128)S(1)}, f32[128,128]{1,0:T(8,128)S(1)}, u32[]{:S(2)}, u32[]{:S(2)}) collective-permute-start(f32[128,128]{1,0:T(8,128)S(1)} %fusion.91), channel_id=1, source_target_pairs={{0,8},{8,16},{16,24},{24,32},{32,40},{40,48},{48,56},{56,64},{64,7... | collective-permute-start | bytes 196616 | tf_op jit(solution)/shard_map/while/body/eval_jaxpr/ppermute | solution.py:14
  380.7 5.9 collective-permute-start.2
  381.0 6.2 %collective-permute-start.3 = (f32[128,128]{1,0:T(8,128)S(1)}, f32[128,128]{1,0:T(8,128)S(1)}, u32[]{:S(2)}, u32[]{:S(2)}) collective-permute-start(f32[128,128]{1,0:T(8,128)S(1)} %fusion.91), channel_id=1, source_target_pairs={{0,8},{8,16},{16,24},{24,32},{32,40},{40,48},{48,56},{56,64},{64,7... | collective-permute-start | bytes 196616 | tf_op jit(solution)/shard_map/while/body/eval_jaxpr/ppermute | solution.py:14
  388.8 5.9 collective-permute-start.2
  389.2 6.2 %collective-permute-start.3 = (f32[128,128]{1,0:T(8,128)S(1)}, f32[128,128]{1,0:T(8,128)S(1)}, u32[]{:S(2)}, u32[]{:S(2)}) collective-permute-start(f32[128,128]{1,0:T(8,128)S(1)} %fusion.91), channel_id=1, source_target_pairs={{0,8},{8,16},{16,24},{24,32},{32,40},{40,48},{48,56},{56,64},{64,7... | collective-permute-start | bytes 196616 | tf_op jit(solution)/shard_map/while/body/eval_jaxpr/ppermute | solution.py:14
  397.0 5.9 collective-permute-start.2
  397.4 6.2 %collective-permute-start.3 = (f32[128,128]{1,0:T(8,128)S(1)}, f32[128,128]{1,0:T(8,128)S(1)}, u32[]{:S(2)}, u32[]{:S(2)}) collective-permute-start(f32[128,128]{1,0:T(8,128)S(1)} %fusion.91), channel_id=1, source_target_pairs={{0,8},{8,16},{16,24},{24,32},{32,40},{40,48},{48,56},{56,64},{64,7... | collective-permute-start | bytes 196616 | tf_op jit(solution)/shard_map/while/body/eval_jaxpr/ppermute | solution.py:14
  405.4 5.9 collective-permute-start.2
  405.8 6.1 %collective-permute-start.3 = (f32[128,128]{1,0:T(8,128)S(1)}, f32[128,128]{1,0:T(8,128)S(1)}, u32[]{:S(2)}, u32[]{:S(2)}) collective-permute-start(f32[128,128]{1,0:T(8,128)S(1)} %fusion.91), channel_id=1, source_target_pairs={{0,8},{8,16},{16,24},{24,32},{32,40},{40,48},{48,56},{56,64},{64,7... | collective-permute-start | bytes 196616 | tf_op jit(solution)/shard_map/while/body/eval_jaxpr/ppermute | solution.py:14
  413.6 5.9 collective-permute-start.2
  414.0 6.1 %collective-permute-start.3 = (f32[128,128]{1,0:T(8,128)S(1)}, f32[128,128]{1,0:T(8,128)S(1)}, u32[]{:S(2)}, u32[]{:S(2)}) collective-permute-start(f32[128,128]{1,0:T(8,128)S(1)} %fusion.91), channel_id=1, source_target_pairs={{0,8},{8,16},{16,24},{24,32},{32,40},{40,48},{48,56},{56,64},{64,7... | collective-permute-start | bytes 196616 | tf_op jit(solution)/shard_map/while/body/eval_jaxpr/ppermute | solution.py:14
  421.8 5.9 collective-permute-start.2
  422.2 6.1 %collective-permute-start.3 = (f32[128,128]{1,0:T(8,128)S(1)}, f32[128,128]{1,0:T(8,128)S(1)}, u32[]{:S(2)}, u32[]{:S(2)}) collective-permute-start(f32[128,128]{1,0:T(8,128)S(1)} %fusion.91), channel_id=1, source_target_pairs={{0,8},{8,16},{16,24},{24,32},{32,40},{40,48},{48,56},{56,64},{64,7... | collective-permute-start | bytes 196616 | tf_op jit(solution)/shard_map/while/body/eval_jaxpr/ppermute | solution.py:14
  429.9 5.9 collective-permute-start.2
  430.4 6.1 %collective-permute-start.3 = (f32[128,128]{1,0:T(8,128)S(1)}, f32[128,128]{1,0:T(8,128)S(1)}, u32[]{:S(2)}, u32[]{:S(2)}) collective-permute-start(f32[128,128]{1,0:T(8,128)S(1)} %fusion.91), channel_id=1, source_target_pairs={{0,8},{8,16},{16,24},{24,32},{32,40},{40,48},{48,56},{56,64},{64,7... | collective-permute-start | bytes 196616 | tf_op jit(solution)/shard_map/while/body/eval_jaxpr/ppermute | solution.py:14
  438.6 6.1 %collective-permute-start.3 = (f32[128,128]{1,0:T(8,128)S(1)}, f32[128,128]{1,0:T(8,128)S(1)}, u32[]{:S(2)}, u32[]{:S(2)}) collective-permute-start(f32[128,128]{1,0:T(8,128)S(1)} %fusion.91), channel_id=1, source_target_pairs={{0,8},{8,16},{16,24},{24,32},{32,40},{40,48},{48,56},{56,64},{64,7... | collective-permute-start | bytes 196616 | tf_op jit(solution)/shard_map/while/body/eval_jaxpr/ppermute | solution.py:14
  446.3 5.9 collective-permute-start.2
  446.7 6.1 %collective-permute-start.3 = (f32[128,128]{1,0:T(8,128)S(1)}, f32[128,128]{1,0:T(8,128)S(1)}, u32[]{:S(2)}, u32[]{:S(2)}) collective-permute-start(f32[128,128]{1,0:T(8,128)S(1)} %fusion.91), channel_id=1, source_target_pairs={{0,8},{8,16},{16,24},{24,32},{32,40},{40,48},{48,56},{56,64},{64,7... | collective-permute-start | bytes 196616 | tf_op jit(solution)/shard_map/while/body/eval_jaxpr/ppermute | solution.py:14
  454.5 5.9 collective-permute-start.2
  454.9 6.1 %collective-permute-start.3 = (f32[128,128]{1,0:T(8,128)S(1)}, f32[128,128]{1,0:T(8,128)S(1)}, u32[]{:S(2)}, u32[]{:S(2)}) collective-permute-start(f32[128,128]{1,0:T(8,128)S(1)} %fusion.91), channel_id=1, source_target_pairs={{0,8},{8,16},{16,24},{24,32},{32,40},{40,48},{48,56},{56,64},{64,7... | collective-permute-start | bytes 196616 | tf_op jit(solution)/shard_map/while/body/eval_jaxpr/ppermute | solution.py:14
  463.1 6.1 %collective-permute-start.3 = (f32[128,128]{1,0:T(8,128)S(1)}, f32[128,128]{1,0:T(8,128)S(1)}, u32[]{:S(2)}, u32[]{:S(2)}) collective-permute-start(f32[128,128]{1,0:T(8,128)S(1)} %fusion.91), channel_id=1, source_target_pairs={{0,8},{8,16},{16,24},{24,32},{32,40},{40,48},{48,56},{56,64},{64,7... | collective-permute-start | bytes 196616 | tf_op jit(solution)/shard_map/while/body/eval_jaxpr/ppermute | solution.py:14
  470.8 5.9 collective-permute-start.2
  471.3 6.1 %collective-permute-start.3 = (f32[128,128]{1,0:T(8,128)S(1)}, f32[128,128]{1,0:T(8,128)S(1)}, u32[]{:S(2)}, u32[]{:S(2)}) collective-permute-start(f32[128,128]{1,0:T(8,128)S(1)} %fusion.91), channel_id=1, source_target_pairs={{0,8},{8,16},{16,24},{24,32},{32,40},{40,48},{48,56},{56,64},{64,7... | collective-permute-start | bytes 196616 | tf_op jit(solution)/shard_map/while/body/eval_jaxpr/ppermute | solution.py:14
  479.0 5.9 collective-permute-start.2
  479.4 6.1 %collective-permute-start.3 = (f32[128,128]{1,0:T(8,128)S(1)}, f32[128,128]{1,0:T(8,128)S(1)}, u32[]{:S(2)}, u32[]{:S(2)}) collective-permute-start(f32[128,128]{1,0:T(8,128)S(1)} %fusion.91), channel_id=1, source_target_pairs={{0,8},{8,16},{16,24},{24,32},{32,40},{40,48},{48,56},{56,64},{64,7... | collective-permute-start | bytes 196616 | tf_op jit(solution)/shard_map/while/body/eval_jaxpr/ppermute | solution.py:14
  487.2 5.9 collective-permute-start.2
  487.6 6.1 %collective-permute-start.3 = (f32[128,128]{1,0:T(8,128)S(1)}, f32[128,128]{1,0:T(8,128)S(1)}, u32[]{:S(2)}, u32[]{:S(2)}) collective-permute-start(f32[128,128]{1,0:T(8,128)S(1)} %fusion.91), channel_id=1, source_target_pairs={{0,8},{8,16},{16,24},{24,32},{32,40},{40,48},{48,56},{56,64},{64,7... | collective-permute-start | bytes 196616 | tf_op jit(solution)/shard_map/while/body/eval_jaxpr/ppermute | solution.py:14
  495.4 5.9 collective-permute-start.2
  495.8 6.1 %collective-permute-start.3 = (f32[128,128]{1,0:T(8,128)S(1)}, f32[128,128]{1,0:T(8,128)S(1)}, u32[]{:S(2)}, u32[]{:S(2)}) collective-permute-start(f32[128,128]{1,0:T(8,128)S(1)} %fusion.91), channel_id=1, source_target_pairs={{0,8},{8,16},{16,24},{24,32},{32,40},{40,48},{48,56},{56,64},{64,7... | collective-permute-start | bytes 196616 | tf_op jit(solution)/shard_map/while/body/eval_jaxpr/ppermute | solution.py:14
  503.5 5.9 collective-permute-start.2
  504.0 6.1 %collective-permute-start.3 = (f32[128,128]{1,0:T(8,128)S(1)}, f32[128,128]{1,0:T(8,128)S(1)}, u32[]{:S(2)}, u32[]{:S(2)}) collective-permute-start(f32[128,128]{1,0:T(8,128)S(1)} %fusion.91), channel_id=1, source_target_pairs={{0,8},{8,16},{16,24},{24,32},{32,40},{40,48},{48,56},{56,64},{64,7... | collective-permute-start | bytes 196616 | tf_op jit(solution)/shard_map/while/body/eval_jaxpr/ppermute | solution.py:14
  511.7 5.9 collective-permute-start.2
  512.2 6.1 %collective-permute-start.3 = (f32[128,128]{1,0:T(8,128)S(1)}, f32[128,128]{1,0:T(8,128)S(1)}, u32[]{:S(2)}, u32[]{:S(2)}) collective-permute-start(f32[128,128]{1,0:T(8,128)S(1)} %fusion.91), channel_id=1, source_target_pairs={{0,8},{8,16},{16,24},{24,32},{32,40},{40,48},{48,56},{56,64},{64,7... | collective-permute-start | bytes 196616 | tf_op jit(solution)/shard_map/while/body/eval_jaxpr/ppermute | solution.py:14
  520.3 6.1 %collective-permute-start.3 = (f32[128,128]{1,0:T(8,128)S(1)}, f32[128,128]{1,0:T(8,128)S(1)}, u32[]{:S(2)}, u32[]{:S(2)}) collective-permute-start(f32[128,128]{1,0:T(8,128)S(1)} %fusion.91), channel_id=1, source_target_pairs={{0,8},{8,16},{16,24},{24,32},{32,40},{40,48},{48,56},{56,64},{64,7... | collective-permute-start | bytes 196616 | tf_op jit(solution)/shard_map/while/body/eval_jaxpr/ppermute | solution.py:14
  528.1 5.9 collective-permute-start.2
  528.5 6.1 %collective-permute-start.3 = (f32[128,128]{1,0:T(8,128)S(1)}, f32[128,128]{1,0:T(8,128)S(1)}, u32[]{:S(2)}, u32[]{:S(2)}) collective-permute-start(f32[128,128]{1,0:T(8,128)S(1)} %fusion.91), channel_id=1, source_target_pairs={{0,8},{8,16},{16,24},{24,32},{32,40},{40,48},{48,56},{56,64},{64,7... | collective-permute-start | bytes 196616 | tf_op jit(solution)/shard_map/while/body/eval_jaxpr/ppermute | solution.py:14
  536.2 5.9 collective-permute-start.2
  536.7 6.1 %collective-permute-start.3 = (f32[128,128]{1,0:T(8,128)S(1)}, f32[128,128]{1,0:T(8,128)S(1)}, u32[]{:S(2)}, u32[]{:S(2)}) collective-permute-start(f32[128,128]{1,0:T(8,128)S(1)} %fusion.91), channel_id=1, source_target_pairs={{0,8},{8,16},{16,24},{24,32},{32,40},{40,48},{48,56},{56,64},{64,7... | collective-permute-start | bytes 196616 | tf_op jit(solution)/shard_map/while/body/eval_jaxpr/ppermute | solution.py:14
  544.9 6.1 %collective-permute-start.3 = (f32[128,128]{1,0:T(8,128)S(1)}, f32[128,128]{1,0:T(8,128)S(1)}, u32[]{:S(2)}, u32[]{:S(2)}) collective-permute-start(f32[128,128]{1,0:T(8,128)S(1)} %fusion.91), channel_id=1, source_target_pairs={{0,8},{8,16},{16,24},{24,32},{32,40},{40,48},{48,56},{56,64},{64,7... | collective-permute-start | bytes 196616 | tf_op jit(solution)/shard_map/while/body/eval_jaxpr/ppermute | solution.py:14
  552.6 5.9 collective-permute-start.2
  553.0 6.1 %collective-permute-start.3 = (f32[128,128]{1,0:T(8,128)S(1)}, f32[128,128]{1,0:T(8,128)S(1)}, u32[]{:S(2)}, u32[]{:S(2)}) collective-permute-start(f32[128,128]{1,0:T(8,128)S(1)} %fusion.91), channel_id=1, source_target_pairs={{0,8},{8,16},{16,24},{24,32},{32,40},{40,48},{48,56},{56,64},{64,7... | collective-permute-start | bytes 196616 | tf_op jit(solution)/shard_map/while/body/eval_jaxpr/ppermute | solution.py:14
  560.8 5.9 collective-permute-start.2
  561.2 6.1 %collective-permute-start.3 = (f32[128,128]{1,0:T(8,128)S(1)}, f32[128,128]{1,0:T(8,128)S(1)}, u32[]{:S(2)}, u32[]{:S(2)}) collective-permute-start(f32[128,128]{1,0:T(8,128)S(1)} %fusion.91), channel_id=1, source_target_pairs={{0,8},{8,16},{16,24},{24,32},{32,40},{40,48},{48,56},{56,64},{64,7... | collective-permute-start | bytes 196616 | tf_op jit(solution)/shard_map/while/body/eval_jaxpr/ppermute | solution.py:14
  568.9 5.9 collective-permute-start.2
  569.4 6.1 %collective-permute-start.3 = (f32[128,128]{1,0:T(8,128)S(1)}, f32[128,128]{1,0:T(8,128)S(1)}, u32[]{:S(2)}, u32[]{:S(2)}) collective-permute-start(f32[128,128]{1,0:T(8,128)S(1)} %fusion.91), channel_id=1, source_target_pairs={{0,8},{8,16},{16,24},{24,32},{32,40},{40,48},{48,56},{56,64},{64,7... | collective-permute-start | bytes 196616 | tf_op jit(solution)/shard_map/while/body/eval_jaxpr/ppermute | solution.py:14
  577.1 5.9 collective-permute-start.2
  577.6 6.1 %collective-permute-start.3 = (f32[128,128]{1,0:T(8,128)S(1)}, f32[128,128]{1,0:T(8,128)S(1)}, u32[]{:S(2)}, u32[]{:S(2)}) collective-permute-start(f32[128,128]{1,0:T(8,128)S(1)} %fusion.91), channel_id=1, source_target_pairs={{0,8},{8,16},{16,24},{24,32},{32,40},{40,48},{48,56},{56,64},{64,7... | collective-permute-start | bytes 196616 | tf_op jit(solution)/shard_map/while/body/eval_jaxpr/ppermute | solution.py:14
  585.3 5.9 collective-permute-start.2
  585.7 6.1 %collective-permute-start.3 = (f32[128,128]{1,0:T(8,128)S(1)}, f32[128,128]{1,0:T(8,128)S(1)}, u32[]{:S(2)}, u32[]{:S(2)}) collective-permute-start(f32[128,128]{1,0:T(8,128)S(1)} %fusion.91), channel_id=1, source_target_pairs={{0,8},{8,16},{16,24},{24,32},{32,40},{40,48},{48,56},{56,64},{64,7... | collective-permute-start | bytes 196616 | tf_op jit(solution)/shard_map/while/body/eval_jaxpr/ppermute | solution.py:14
  593.5 5.9 collective-permute-start.2
  593.9 6.1 %collective-permute-start.3 = (f32[128,128]{1,0:T(8,128)S(1)}, f32[128,128]{1,0:T(8,128)S(1)}, u32[]{:S(2)}, u32[]{:S(2)}) collective-permute-start(f32[128,128]{1,0:T(8,128)S(1)} %fusion.91), channel_id=1, source_target_pairs={{0,8},{8,16},{16,24},{24,32},{32,40},{40,48},{48,56},{56,64},{64,7... | collective-permute-start | bytes 196616 | tf_op jit(solution)/shard_map/while/body/eval_jaxpr/ppermute | solution.py:14
  (71 other events, 512.7 us)
Sparse Core Ops, SparseCore 0:
  10.4 66.7 all-gather.4
  79.8 59.4 all-gather.6
  141.1 121.8 all-gather.8
  265.3 62.7 all-gather.10
where the time goes:
time: 610 us; the launch traced here: 609 us
  waiting for transfers between devices  383 us (63%)
  matrix products  84.8 us (14%)
  starting transfers between devices  73.6 us (12%)
  other arithmetic  36.2 us (6%)
  local copies, waits for them, and re-layouts  14.8 us (2%)
  between operations  14 us (2%)
    all_gather x1, waiting for transfers between devices, per_device(): lax.all_gather(w_out, 'ctx', axis=1, tiled=True)  124 us
    ppermute x128, waiting for transfers between devices, shifted(): return lax.ppermute(value, axis, pairs)  124 us
    ppermute x128, starting transfers between devices, shifted(): return lax.ppermute(value, axis, pairs)  73.5 us
    all_gather x1, waiting for transfers between devices, per_device(): value_piece = lax.all_gather(value, 'ctx', axis=0, tiled=True)  52.8 us
    all_gather x1, waiting for transfers between devices, per_device(): full_rows = lax.all_gather(grad_y, 'head', axis=1, tiled=True)  47.1 us
    all_gather x1, waiting for transfers between devices, per_device(): key_piece = lax.all_gather(key_in, 'ctx', axis=0, tiled=True)  33.4 us
    reduce_sum x32, other arithmetic, advance(): jnp.sum(jnp.where(current[:, None] == index[None, :], parent[None, :], 0)...  26.9 us
    dot_general x32, matrix products, contribution(): jnp.einsum('ghqd,gkd->ghqk', query_heads, key_heads, preferred_element_ty...  17.2 us
  transfers between devices with their start and end apart: 132, of which 132 were waited for; matrix products, arithmetic and copies ran while one was open for 19% of the time, Pallas kernels for 0%

commit v1 on v0

--- a/solution.py
+++ b/solution.py
@@ -73,7 +73,10 @@
         return tensor.transpose(1, 0, 2).reshape(tensor.shape[1], groups * DH)
 
     stat_shape = (groups, HPG, tokens_here)
-    key_piece = lax.all_gather(key_in, "ctx", axis=0, tiled=True)
+    draw_cubes_over_axis = lambda panel, axis_key: jnp.concatenate(
+        lax.all_to_all(jnp.stack([panel] * lax.axis_size(axis_key)), axis_key, 0, 0), axis=0
+    )
+    key_piece = draw_cubes_over_axis(key_in, "ctx")
     value_piece = lax.all_gather(value, "ctx", axis=0, tiled=True)
     mask = make_mask(jnp.int32(0), key_piece.shape[0])
     statistics_top = jnp.full(stat_shape, -1e30, jnp.float32)

time: 610 us -> 546 us (0.90)
  waiting for transfers between devices: 383 us -> 310 us
  starting transfers between devices: 73.6 us -> 83.4 us
    all_gather x1, waiting for transfers between devices: 47.1 us -> 7.81 us  [per_device(): full_rows = lax.all_gather(grad_y, 'head', axis=1, tiled=True)]
    all_gather x1 -> x0, waiting for transfers between devices: 33.4 us -> none  [per_device(): key_piece = lax.all_gather(key_in, 'ctx', axis=0, tiled=True)]
    all_to_all x0 -> x1, starting transfers between devices: none -> 9.87 us  [per_device(): lax.all_to_all(jnp.stack([panel] * lax.axis_size(axis_key)), axis_key, 0, 0)]
  transfers between devices with their start and end apart: 132 -> 132, of which waited for: 132 -> 131; matrix products, arithmetic and copies ran while one was open for 19% -> 21% of each run, Pallas kernels for 0% -> 0%
where the time goes in v1:
time: 546 us; the launch traced here: 545 us
  waiting for transfers between devices  310 us (57%)
  matrix products  83.5 us (15%)
  starting transfers between devices  83.4 us (15%)
  other arithmetic  36.3 us (7%)
  local copies, waits for them, and re-layouts  15.4 us (3%)
  between operations  13.9 us (3%)
    all_gather x1, waiting for transfers between devices, per_device(): lax.all_gather(w_out, 'ctx', axis=1, tiled=True)  124 us
    ppermute x128, waiting for transfers between devices, shifted(): return lax.ppermute(value, axis, pairs)  124 us
    ppermute x128, starting transfers between devices, shifted(): return lax.ppermute(value, axis, pairs)  73.5 us
    all_gather x1, waiting for transfers between devices, per_device(): value_piece = lax.all_gather(value, 'ctx', axis=0, tiled=True)  53 us
    reduce_sum x32, other arithmetic, advance(): jnp.sum(jnp.where(current[:, None] == index[None, :], parent[None, :], 0)...  26.9 us
    dot_general x32, matrix products, contribution(): jnp.einsum('ghqd,gkd->ghqk', query_heads, key_heads, preferred_element_ty...  17.2 us
    dot_general x1, matrix products, per_device(): lax.dot_general(full_rows, lax.all_gather(w_out, 'ctx', axis=1, tiled=Tru...  12.1 us
  transfers between devices with their start and end apart: 132, of which 131 were waited for; matrix products, arithmetic and copies ran while one was open for 21% of the time, Pallas kernels for 0%

profile of v1, /device:TPU:2, one launch (start us, length us, event | category | flops | bytes accessed | tf_op | source)
XLA Modules:
  0.0 544.9 jit_solution(16485146466728743652)
XLA Ops:
  11.3 9.9 %all-to-all-start = ((bf16[32,128,128]{2,1,0:T(8,128)(2,1)}), bf16[32,128,128]{2,1,0:T(8,128)(2,1)S(1)}, u32[]{:S(2)}, u32[]{:S(2)}) async-start(bf16[32,128,128]{2,1,0:T(8,128)(2,1)} %stack.2), calls=%async_computation | async-start | bytes 2097152 | tf_op jit(solution)/shard_map/all_to_all | solution.py:77
  22.0 29.5 %while.40 = (s32[]{:T(128)}, s32[32]{0:T(128)S(1)}, s32[32,32]{1,0:T(8,128)S(1)}, s32[32]{0:T(128)}, s32[]{:T(128)}) while((s32[]{:T(128)}, s32[32]{0:T(128)S(1)}, s32[32,32]{1,0:T(8,128)S(1)}, s32[32]{0:T(128)}, s32[]{:T(128)}) %tuple.80), condition=%wide.region_2.3_spmd.clone.clone, body=%wide.region_0.2_spmd.clone.clone.sunk | while | flops 6114 | bytes 9021 | solution.py:28
  53.6 3.2 select_reduce_fusion.1
  56.8 5.7 %copy-done = f32[8,128,4096]{2,1,0:T(8,128)} copy-done((f32[8,128,4096]{2,1,0:T(8,128)}, f32[8,128,4096]{2,1,0:T(8,128)S(1)}, u32[]{:S(2)}) %copy-start) | copy-done | bytes 16777240
  62.5 4.9 fusion.35
  67.5 7.8 %all-gather.4.cloned.1.call-done = bf16[128,8192]{1,0:T(8,128)(2,1)} async-done(((bf16[128,1024]{1,0:T(8,128)(2,1)}), bf16[128,8192]{1,0:T(8,128)(2,1)}) %all-gather.4.cloned.1.call-update) | async-done | bytes 2097168 | tf_op jit(solution)/shard_map/all_gather | solution.py:37
  75.3 123.7 %all-gather.6.cloned.1.call-done = bf16[1024,8192]{1,0:T(8,128)(2,1)} async-done(((bf16[1024,256]{1,0:T(8,128)(2,1)}), bf16[1024,8192]{1,0:T(8,128)(2,1)}) %all-gather.6.cloned.1.call-update) | async-done | bytes 16777232 | tf_op jit(solution)/shard_map/all_gather | solution.py:40
  199.0 12.1 %fusion.38 = bf16[16,8,8,128]{3,1,2,0:T(8,128)(2,1)S(1)} fusion(bf16[128,8192]{1,0:T(8,128)(2,1)} %all-gather.4.cloned.1.call-done, bf16[1024,8192]{1,0:T(8,128)(2,1)} %all-gather.6.cloned.1.call-done), kind=kOutput, calls=%fused_computation.60 | convolution fusion | flops 2147614720 | bytes 19136512 | tf_op jit(solution)/shard_map/dot_general | solution.py:38
  211.2 53.0 %all-gather.8.cloned.1.call-done = bf16[4096,128]{1,0:T(8,128)(2,1)} async-done(((bf16[128,128]{1,0:T(8,128)(2,1)}), bf16[4096,128]{1,0:T(8,128)(2,1)}) %all-gather.8.cloned.1.call-update) | async-done | bytes 1048592 | tf_op jit(solution)/shard_map/all_gather | solution.py:80
  264.2 9.0 %multiply_reduce_fusion = f32[8,128]{1,0:T(8,128)S(1)} fusion(f32[8,128,4096]{2,1,0:T(8,128)} %copy-done, f32[8,128]{1,0:T(8,128)S(1)} %get-tuple-element.648, pred[128,4096]{1,0:T(8,128)(4,1)S(1)} %fusion.36, bf16[4096,128]{1,0:T(8,128)(2,1)} %all-gather.8.cloned.1.call-done, bf16[128,1,8,128]{3,2,0,1:T(8,128)(2,1)S(1)} %bitcast.121), kind=kOutput, calls=%fused_computation.51 | convolution fusion | flops 1094712320 | bytes 18620416 | tf_op jit(solution)/shard_map/ghqd,gkd->ghqk/dot_general | solution.py:95
  273.2 263.0 %while.41 = (s32[]{:T(128)}, f32[1,8,128,128]{3,2,1,0:T(8,128)S(1)}, bf16[128,128]{1,0:T(8,128)(2,1)S(1)}, bf16[128,128]{1,0:T(8,128)(2,1)S(1)}, f32[128,128]{1,...) while((s32[]{:T(128)}, ...), condition=%wide.region_7.8_spmd.clone.clone.clone, body=%wide.region_6.7_spmd.clone.clone.clone.sunk | while | flops 170405904 | bytes 5817452 | solution.py:150
  279.3 2.5 collective-permute-done.2
  288.3 1.7 collective-permute-done.2
  296.5 1.7 collective-permute-done.2
  300.8 1.8 collective-permute-start.3
  304.7 1.7 collective-permute-done.2
  309.9 2.6 collective-permute-done.1
  312.8 1.7 collective-permute-done.2
  318.0 2.7 collective-permute-done.1
  321.0 1.7 collective-permute-done.2
  326.7 2.2 collective-permute-done.1
  329.2 1.7 collective-permute-done.2
  333.5 2.5 collective-permute-start.3
  337.4 1.7 collective-permute-done.2
  342.0 2.2 collective-permute-start.3
  345.6 1.9 collective-permute-done.2
  350.2 2.2 collective-permute-start.3
  353.9 1.7 collective-permute-done.2
  358.3 2.2 collective-permute-start.3
  362.1 1.7 collective-permute-done.2
  366.5 2.2 collective-permute-start.3
  370.3 1.7 collective-permute-done.2
  374.7 2.2 collective-permute-start.3
  378.5 1.7 collective-permute-done.2
  382.9 2.2 collective-permute-start.3
  391.0 2.2 collective-permute-start.3
  394.8 1.7 collective-permute-done.2
  399.2 2.2 collective-permute-start.3
  407.4 2.2 collective-permute-start.3
  411.2 1.7 collective-permute-done.2
  415.6 2.2 collective-permute-start.3
  423.8 2.2 collective-permute-start.3
  427.5 1.7 collective-permute-done.2
  431.9 2.2 collective-permute-start.3
  435.7 1.7 collective-permute-done.2
  440.1 2.2 collective-permute-start.3
  443.9 1.7 collective-permute-done.2
  448.3 2.2 collective-permute-start.3
  452.1 1.7 collective-permute-done.2
  456.5 2.2 collective-permute-start.3
  460.2 1.7 collective-permute-done.2
  464.6 2.2 collective-permute-start.3
  472.8 2.2 collective-permute-start.3
  476.6 1.7 collective-permute-done.2
  481.0 2.2 collective-permute-start.3
  489.2 2.2 collective-permute-start.3
  492.9 1.7 collective-permute-done.2
  497.4 2.2 collective-permute-start.3
  505.5 2.2 collective-permute-start.3
  509.3 1.7 collective-permute-done.2
  513.7 2.2 collective-permute-start.3
  521.9 2.2 collective-permute-start.3
  525.6 1.7 collective-permute-done.2
  530.1 2.2 collective-permute-start.3
  (685 shorter events, 192.8 us)
Async XLA Ops:
  7.2 68.1 %all-gather.4.cloned.1.call-start = ((), (), s32[]{:S(2)}) async-start(), calls=%async_computation.1 | async-start | bytes 2359296 | tf_op jit(solution)/shard_map/all_gather | solution.py:37
  9.4 189.6 %all-gather.6.cloned.1.call-start = ((), (), s32[]{:S(2)}) async-start(), calls=%async_computation.2 | async-start | bytes 17301504 | tf_op jit(solution)/shard_map/all_gather | solution.py:40
  11.3 42.3 %all-to-all-start = ((bf16[32,128,128]{2,1,0:T(8,128)(2,1)}), bf16[32,128,128]{2,1,0:T(8,128)(2,1)S(1)}, u32[]{:S(2)}, u32[]{:S(2)}) async-start(bf16[32,128,128]{2,1,0:T(8,128)(2,1)} %stack.2), calls=%async_computation | async-start | bytes 2097152 | tf_op jit(solution)/shard_map/all_to_all | solution.py:77
  21.2 243.0 %all-gather.8.cloned.1.call-start = ((), (), s32[]{:S(2)}) async-start(), calls=%async_computation.3 | async-start | bytes 1081344 | tf_op jit(solution)/shard_map/all_gather | solution.py:80
  275.9 5.9 %collective-permute-start.2 = (f32[128,128]{1,0:T(8,128)S(1)}, f32[128,128]{1,0:T(8,128)S(1)}, u32[]{:S(2)}, u32[]{:S(2)}) collective-permute-start(f32[128,128]{1,0:T(8,128)S(1)} %fusion.89), channel_id=1, source_target_pairs={{0,8},{8,16},{16,24},{24,32},{32,40},{40,48},{48,56},{56,64},{64,7... | collective-permute-start | bytes 196616 | tf_op jit(solution)/shard_map/while/body/eval_jaxpr/ppermute | solution.py:14
  276.5 6.0 %collective-permute-start.3 = (f32[128,128]{1,0:T(8,128)S(1)}, f32[128,128]{1,0:T(8,128)S(1)}, u32[]{:S(2)}, u32[]{:S(2)}) collective-permute-start(f32[128,128]{1,0:T(8,128)S(1)} %fusion.90), channel_id=1, source_target_pairs={{0,8},{8,16},{16,24},{24,32},{32,40},{40,48},{48,56},{56,64},{64,7... | collective-permute-start | bytes 196616 | tf_op jit(solution)/shard_map/while/body/eval_jaxpr/ppermute | solution.py:14
  284.1 5.9 %collective-permute-start.2 = (f32[128,128]{1,0:T(8,128)S(1)}, f32[128,128]{1,0:T(8,128)S(1)}, u32[]{:S(2)}, u32[]{:S(2)}) collective-permute-start(f32[128,128]{1,0:T(8,128)S(1)} %fusion.89), channel_id=1, source_target_pairs={{0,8},{8,16},{16,24},{24,32},{32,40},{40,48},{48,56},{56,64},{64,7... | collective-permute-start | bytes 196616 | tf_op jit(solution)/shard_map/while/body/eval_jaxpr/ppermute | solution.py:14
  284.5 6.2 %collective-permute-start.3 = (f32[128,128]{1,0:T(8,128)S(1)}, f32[128,128]{1,0:T(8,128)S(1)}, u32[]{:S(2)}, u32[]{:S(2)}) collective-permute-start(f32[128,128]{1,0:T(8,128)S(1)} %fusion.90), channel_id=1, source_target_pairs={{0,8},{8,16},{16,24},{24,32},{32,40},{40,48},{48,56},{56,64},{64,7... | collective-permute-start | bytes 196616 | tf_op jit(solution)/shard_map/while/body/eval_jaxpr/ppermute | solution.py:14
  292.3 5.9 %collective-permute-start.2 = (f32[128,128]{1,0:T(8,128)S(1)}, f32[128,128]{1,0:T(8,128)S(1)}, u32[]{:S(2)}, u32[]{:S(2)}) collective-permute-start(f32[128,128]{1,0:T(8,128)S(1)} %fusion.89), channel_id=1, source_target_pairs={{0,8},{8,16},{16,24},{24,32},{32,40},{40,48},{48,56},{56,64},{64,7... | collective-permute-start | bytes 196616 | tf_op jit(solution)/shard_map/while/body/eval_jaxpr/ppermute | solution.py:14
  292.7 6.2 %collective-permute-start.3 = (f32[128,128]{1,0:T(8,128)S(1)}, f32[128,128]{1,0:T(8,128)S(1)}, u32[]{:S(2)}, u32[]{:S(2)}) collective-permute-start(f32[128,128]{1,0:T(8,128)S(1)} %fusion.90), channel_id=1, source_target_pairs={{0,8},{8,16},{16,24},{24,32},{32,40},{40,48},{48,56},{56,64},{64,7... | collective-permute-start | bytes 196616 | tf_op jit(solution)/shard_map/while/body/eval_jaxpr/ppermute | solution.py:14
  300.5 5.9 %collective-permute-start.2 = (f32[128,128]{1,0:T(8,128)S(1)}, f32[128,128]{1,0:T(8,128)S(1)}, u32[]{:S(2)}, u32[]{:S(2)}) collective-permute-start(f32[128,128]{1,0:T(8,128)S(1)} %fusion.89), channel_id=1, source_target_pairs={{0,8},{8,16},{16,24},{24,32},{32,40},{40,48},{48,56},{56,64},{64,7... | collective-permute-start | bytes 196616 | tf_op jit(solution)/shard_map/while/body/eval_jaxpr/ppermute | solution.py:14
  300.8 6.2 %collective-permute-start.3 = (f32[128,128]{1,0:T(8,128)S(1)}, f32[128,128]{1,0:T(8,128)S(1)}, u32[]{:S(2)}, u32[]{:S(2)}) collective-permute-start(f32[128,128]{1,0:T(8,128)S(1)} %fusion.90), channel_id=1, source_target_pairs={{0,8},{8,16},{16,24},{24,32},{32,40},{40,48},{48,56},{56,64},{64,7... | collective-permute-start | bytes 196616 | tf_op jit(solution)/shard_map/while/body/eval_jaxpr/ppermute | solution.py:14
  308.6 5.9 %collective-permute-start.2 = (f32[128,128]{1,0:T(8,128)S(1)}, f32[128,128]{1,0:T(8,128)S(1)}, u32[]{:S(2)}, u32[]{:S(2)}) collective-permute-start(f32[128,128]{1,0:T(8,128)S(1)} %fusion.89), channel_id=1, source_target_pairs={{0,8},{8,16},{16,24},{24,32},{32,40},{40,48},{48,56},{56,64},{64,7... | collective-permute-start | bytes 196616 | tf_op jit(solution)/shard_map/while/body/eval_jaxpr/ppermute | solution.py:14
  309.0 6.2 %collective-permute-start.3 = (f32[128,128]{1,0:T(8,128)S(1)}, f32[128,128]{1,0:T(8,128)S(1)}, u32[]{:S(2)}, u32[]{:S(2)}) collective-permute-start(f32[128,128]{1,0:T(8,128)S(1)} %fusion.90), channel_id=1, source_target_pairs={{0,8},{8,16},{16,24},{24,32},{32,40},{40,48},{48,56},{56,64},{64,7... | collective-permute-start | bytes 196616 | tf_op jit(solution)/shard_map/while/body/eval_jaxpr/ppermute | solution.py:14
  316.8 5.9 %collective-permute-start.2 = (f32[128,128]{1,0:T(8,128)S(1)}, f32[128,128]{1,0:T(8,128)S(1)}, u32[]{:S(2)}, u32[]{:S(2)}) collective-permute-start(f32[128,128]{1,0:T(8,128)S(1)} %fusion.89), channel_id=1, source_target_pairs={{0,8},{8,16},{16,24},{24,32},{32,40},{40,48},{48,56},{56,64},{64,7... | collective-permute-start | bytes 196616 | tf_op jit(solution)/shard_map/while/body/eval_jaxpr/ppermute | solution.py:14
  317.2 6.2 %collective-permute-start.3 = (f32[128,128]{1,0:T(8,128)S(1)}, f32[128,128]{1,0:T(8,128)S(1)}, u32[]{:S(2)}, u32[]{:S(2)}) collective-permute-start(f32[128,128]{1,0:T(8,128)S(1)} %fusion.90), channel_id=1, source_target_pairs={{0,8},{8,16},{16,24},{24,32},{32,40},{40,48},{48,56},{56,64},{64,7... | collective-permute-start | bytes 196616 | tf_op jit(solution)/shard_map/while/body/eval_jaxpr/ppermute | solution.py:14
  325.0 5.9 %collective-permute-start.2 = (f32[128,128]{1,0:T(8,128)S(1)}, f32[128,128]{1,0:T(8,128)S(1)}, u32[]{:S(2)}, u32[]{:S(2)}) collective-permute-start(f32[128,128]{1,0:T(8,128)S(1)} %fusion.89), channel_id=1, source_target_pairs={{0,8},{8,16},{16,24},{24,32},{32,40},{40,48},{48,56},{56,64},{64,7... | collective-permute-start | bytes 196616 | tf_op jit(solution)/shard_map/while/body/eval_jaxpr/ppermute | solution.py:14
  325.4 6.2 %collective-permute-start.3 = (f32[128,128]{1,0:T(8,128)S(1)}, f32[128,128]{1,0:T(8,128)S(1)}, u32[]{:S(2)}, u32[]{:S(2)}) collective-permute-start(f32[128,128]{1,0:T(8,128)S(1)} %fusion.90), channel_id=1, source_target_pairs={{0,8},{8,16},{16,24},{24,32},{32,40},{40,48},{48,56},{56,64},{64,7... | collective-permute-start | bytes 196616 | tf_op jit(solution)/shard_map/while/body/eval_jaxpr/ppermute | solution.py:14
  333.2 5.9 %collective-permute-start.2 = (f32[128,128]{1,0:T(8,128)S(1)}, f32[128,128]{1,0:T(8,128)S(1)}, u32[]{:S(2)}, u32[]{:S(2)}) collective-permute-start(f32[128,128]{1,0:T(8,128)S(1)} %fusion.89), channel_id=1, source_target_pairs={{0,8},{8,16},{16,24},{24,32},{32,40},{40,48},{48,56},{56,64},{64,7... | collective-permute-start | bytes 196616 | tf_op jit(solution)/shard_map/while/body/eval_jaxpr/ppermute | solution.py:14
  333.5 6.2 %collective-permute-start.3 = (f32[128,128]{1,0:T(8,128)S(1)}, f32[128,128]{1,0:T(8,128)S(1)}, u32[]{:S(2)}, u32[]{:S(2)}) collective-permute-start(f32[128,128]{1,0:T(8,128)S(1)} %fusion.90), channel_id=1, source_target_pairs={{0,8},{8,16},{16,24},{24,32},{32,40},{40,48},{48,56},{56,64},{64,7... | collective-permute-start | bytes 196616 | tf_op jit(solution)/shard_map/while/body/eval_jaxpr/ppermute | solution.py:14
  341.5 5.9 %collective-permute-start.2 = (f32[128,128]{1,0:T(8,128)S(1)}, f32[128,128]{1,0:T(8,128)S(1)}, u32[]{:S(2)}, u32[]{:S(2)}) collective-permute-start(f32[128,128]{1,0:T(8,128)S(1)} %fusion.89), channel_id=1, source_target_pairs={{0,8},{8,16},{16,24},{24,32},{32,40},{40,48},{48,56},{56,64},{64,7... | collective-permute-start | bytes 196616 | tf_op jit(solution)/shard_map/while/body/eval_jaxpr/ppermute | solution.py:14
  342.0 6.1 %collective-permute-start.3 = (f32[128,128]{1,0:T(8,128)S(1)}, f32[128,128]{1,0:T(8,128)S(1)}, u32[]{:S(2)}, u32[]{:S(2)}) collective-permute-start(f32[128,128]{1,0:T(8,128)S(1)} %fusion.90), channel_id=1, source_target_pairs={{0,8},{8,16},{16,24},{24,32},{32,40},{40,48},{48,56},{56,64},{64,7... | collective-permute-start | bytes 196616 | tf_op jit(solution)/shard_map/while/body/eval_jaxpr/ppermute | solution.py:14
  349.7 5.9 %collective-permute-start.2 = (f32[128,128]{1,0:T(8,128)S(1)}, f32[128,128]{1,0:T(8,128)S(1)}, u32[]{:S(2)}, u32[]{:S(2)}) collective-permute-start(f32[128,128]{1,0:T(8,128)S(1)} %fusion.89), channel_id=1, source_target_pairs={{0,8},{8,16},{16,24},{24,32},{32,40},{40,48},{48,56},{56,64},{64,7... | collective-permute-start | bytes 196616 | tf_op jit(solution)/shard_map/while/body/eval_jaxpr/ppermute | solution.py:14
  350.2 6.1 %collective-permute-start.3 = (f32[128,128]{1,0:T(8,128)S(1)}, f32[128,128]{1,0:T(8,128)S(1)}, u32[]{:S(2)}, u32[]{:S(2)}) collective-permute-start(f32[128,128]{1,0:T(8,128)S(1)} %fusion.90), channel_id=1, source_target_pairs={{0,8},{8,16},{16,24},{24,32},{32,40},{40,48},{48,56},{56,64},{64,7... | collective-permute-start | bytes 196616 | tf_op jit(solution)/shard_map/while/body/eval_jaxpr/ppermute | solution.py:14
  357.9 5.9 %collective-permute-start.2 = (f32[128,128]{1,0:T(8,128)S(1)}, f32[128,128]{1,0:T(8,128)S(1)}, u32[]{:S(2)}, u32[]{:S(2)}) collective-permute-start(f32[128,128]{1,0:T(8,128)S(1)} %fusion.89), channel_id=1, source_target_pairs={{0,8},{8,16},{16,24},{24,32},{32,40},{40,48},{48,56},{56,64},{64,7... | collective-permute-start | bytes 196616 | tf_op jit(solution)/shard_map/while/body/eval_jaxpr/ppermute | solution.py:14
  358.3 6.1 %collective-permute-start.3 = (f32[128,128]{1,0:T(8,128)S(1)}, f32[128,128]{1,0:T(8,128)S(1)}, u32[]{:S(2)}, u32[]{:S(2)}) collective-permute-start(f32[128,128]{1,0:T(8,128)S(1)} %fusion.90), channel_id=1, source_target_pairs={{0,8},{8,16},{16,24},{24,32},{32,40},{40,48},{48,56},{56,64},{64,7... | collective-permute-start | bytes 196616 | tf_op jit(solution)/shard_map/while/body/eval_jaxpr/ppermute | solution.py:14
  366.1 5.9 %collective-permute-start.2 = (f32[128,128]{1,0:T(8,128)S(1)}, f32[128,128]{1,0:T(8,128)S(1)}, u32[]{:S(2)}, u32[]{:S(2)}) collective-permute-start(f32[128,128]{1,0:T(8,128)S(1)} %fusion.89), channel_id=1, source_target_pairs={{0,8},{8,16},{16,24},{24,32},{32,40},{40,48},{48,56},{56,64},{64,7... | collective-permute-start | bytes 196616 | tf_op jit(solution)/shard_map/while/body/eval_jaxpr/ppermute | solution.py:14
  366.5 6.1 %collective-permute-start.3 = (f32[128,128]{1,0:T(8,128)S(1)}, f32[128,128]{1,0:T(8,128)S(1)}, u32[]{:S(2)}, u32[]{:S(2)}) collective-permute-start(f32[128,128]{1,0:T(8,128)S(1)} %fusion.90), channel_id=1, source_target_pairs={{0,8},{8,16},{16,24},{24,32},{32,40},{40,48},{48,56},{56,64},{64,7... | collective-permute-start | bytes 196616 | tf_op jit(solution)/shard_map/while/body/eval_jaxpr/ppermute | solution.py:14
  374.3 5.9 %collective-permute-start.2 = (f32[128,128]{1,0:T(8,128)S(1)}, f32[128,128]{1,0:T(8,128)S(1)}, u32[]{:S(2)}, u32[]{:S(2)}) collective-permute-start(f32[128,128]{1,0:T(8,128)S(1)} %fusion.89), channel_id=1, source_target_pairs={{0,8},{8,16},{16,24},{24,32},{32,40},{40,48},{48,56},{56,64},{64,7... | collective-permute-start | bytes 196616 | tf_op jit(solution)/shard_map/while/body/eval_jaxpr/ppermute | solution.py:14
  374.7 6.1 %collective-permute-start.3 = (f32[128,128]{1,0:T(8,128)S(1)}, f32[128,128]{1,0:T(8,128)S(1)}, u32[]{:S(2)}, u32[]{:S(2)}) collective-permute-start(f32[128,128]{1,0:T(8,128)S(1)} %fusion.90), channel_id=1, source_target_pairs={{0,8},{8,16},{16,24},{24,32},{32,40},{40,48},{48,56},{56,64},{64,7... | collective-permute-start | bytes 196616 | tf_op jit(solution)/shard_map/while/body/eval_jaxpr/ppermute | solution.py:14
  382.4 5.9 %collective-permute-start.2 = (f32[128,128]{1,0:T(8,128)S(1)}, f32[128,128]{1,0:T(8,128)S(1)}, u32[]{:S(2)}, u32[]{:S(2)}) collective-permute-start(f32[128,128]{1,0:T(8,128)S(1)} %fusion.89), channel_id=1, source_target_pairs={{0,8},{8,16},{16,24},{24,32},{32,40},{40,48},{48,56},{56,64},{64,7... | collective-permute-start | bytes 196616 | tf_op jit(solution)/shard_map/while/body/eval_jaxpr/ppermute | solution.py:14
  382.9 6.1 %collective-permute-start.3 = (f32[128,128]{1,0:T(8,128)S(1)}, f32[128,128]{1,0:T(8,128)S(1)}, u32[]{:S(2)}, u32[]{:S(2)}) collective-permute-start(f32[128,128]{1,0:T(8,128)S(1)} %fusion.90), channel_id=1, source_target_pairs={{0,8},{8,16},{16,24},{24,32},{32,40},{40,48},{48,56},{56,64},{64,7... | collective-permute-start | bytes 196616 | tf_op jit(solution)/shard_map/while/body/eval_jaxpr/ppermute | solution.py:14
  390.6 5.9 %collective-permute-start.2 = (f32[128,128]{1,0:T(8,128)S(1)}, f32[128,128]{1,0:T(8,128)S(1)}, u32[]{:S(2)}, u32[]{:S(2)}) collective-permute-start(f32[128,128]{1,0:T(8,128)S(1)} %fusion.89), channel_id=1, source_target_pairs={{0,8},{8,16},{16,24},{24,32},{32,40},{40,48},{48,56},{56,64},{64,7... | collective-permute-start | bytes 196616 | tf_op jit(solution)/shard_map/while/body/eval_jaxpr/ppermute | solution.py:14
  391.0 6.1 %collective-permute-start.3 = (f32[128,128]{1,0:T(8,128)S(1)}, f32[128,128]{1,0:T(8,128)S(1)}, u32[]{:S(2)}, u32[]{:S(2)}) collective-permute-start(f32[128,128]{1,0:T(8,128)S(1)} %fusion.90), channel_id=1, source_target_pairs={{0,8},{8,16},{16,24},{24,32},{32,40},{40,48},{48,56},{56,64},{64,7... | collective-permute-start | bytes 196616 | tf_op jit(solution)/shard_map/while/body/eval_jaxpr/ppermute | solution.py:14
  398.8 5.9 %collective-permute-start.2 = (f32[128,128]{1,0:T(8,128)S(1)}, f32[128,128]{1,0:T(8,128)S(1)}, u32[]{:S(2)}, u32[]{:S(2)}) collective-permute-start(f32[128,128]{1,0:T(8,128)S(1)} %fusion.89), channel_id=1, source_target_pairs={{0,8},{8,16},{16,24},{24,32},{32,40},{40,48},{48,56},{56,64},{64,7... | collective-permute-start | bytes 196616 | tf_op jit(solution)/shard_map/while/body/eval_jaxpr/ppermute | solution.py:14
  399.2 6.1 %collective-permute-start.3 = (f32[128,128]{1,0:T(8,128)S(1)}, f32[128,128]{1,0:T(8,128)S(1)}, u32[]{:S(2)}, u32[]{:S(2)}) collective-permute-start(f32[128,128]{1,0:T(8,128)S(1)} %fusion.90), channel_id=1, source_target_pairs={{0,8},{8,16},{16,24},{24,32},{32,40},{40,48},{48,56},{56,64},{64,7... | collective-permute-start | bytes 196616 | tf_op jit(solution)/shard_map/while/body/eval_jaxpr/ppermute | solution.py:14
  407.0 5.9 %collective-permute-start.2 = (f32[128,128]{1,0:T(8,128)S(1)}, f32[128,128]{1,0:T(8,128)S(1)}, u32[]{:S(2)}, u32[]{:S(2)}) collective-permute-start(f32[128,128]{1,0:T(8,128)S(1)} %fusion.89), channel_id=1, source_target_pairs={{0,8},{8,16},{16,24},{24,32},{32,40},{40,48},{48,56},{56,64},{64,7... | collective-permute-start | bytes 196616 | tf_op jit(solution)/shard_map/while/body/eval_jaxpr/ppermute | solution.py:14
  407.4 6.1 %collective-permute-start.3 = (f32[128,128]{1,0:T(8,128)S(1)}, f32[128,128]{1,0:T(8,128)S(1)}, u32[]{:S(2)}, u32[]{:S(2)}) collective-permute-start(f32[128,128]{1,0:T(8,128)S(1)} %fusion.90), channel_id=1, source_target_pairs={{0,8},{8,16},{16,24},{24,32},{32,40},{40,48},{48,56},{56,64},{64,7... | collective-permute-start | bytes 196616 | tf_op jit(solution)/shard_map/while/body/eval_jaxpr/ppermute | solution.py:14
  415.1 5.9 %collective-permute-start.2 = (f32[128,128]{1,0:T(8,128)S(1)}, f32[128,128]{1,0:T(8,128)S(1)}, u32[]{:S(2)}, u32[]{:S(2)}) collective-permute-start(f32[128,128]{1,0:T(8,128)S(1)} %fusion.89), channel_id=1, source_target_pairs={{0,8},{8,16},{16,24},{24,32},{32,40},{40,48},{48,56},{56,64},{64,7... | collective-permute-start | bytes 196616 | tf_op jit(solution)/shard_map/while/body/eval_jaxpr/ppermute | solution.py:14
  415.6 6.1 %collective-permute-start.3 = (f32[128,128]{1,0:T(8,128)S(1)}, f32[128,128]{1,0:T(8,128)S(1)}, u32[]{:S(2)}, u32[]{:S(2)}) collective-permute-start(f32[128,128]{1,0:T(8,128)S(1)} %fusion.90), channel_id=1, source_target_pairs={{0,8},{8,16},{16,24},{24,32},{32,40},{40,48},{48,56},{56,64},{64,7... | collective-permute-start | bytes 196616 | tf_op jit(solution)/shard_map/while/body/eval_jaxpr/ppermute | solution.py:14
  423.3 5.9 %collective-permute-start.2 = (f32[128,128]{1,0:T(8,128)S(1)}, f32[128,128]{1,0:T(8,128)S(1)}, u32[]{:S(2)}, u32[]{:S(2)}) collective-permute-start(f32[128,128]{1,0:T(8,128)S(1)} %fusion.89), channel_id=1, source_target_pairs={{0,8},{8,16},{16,24},{24,32},{32,40},{40,48},{48,56},{56,64},{64,7... | collective-permute-start | bytes 196616 | tf_op jit(solution)/shard_map/while/body/eval_jaxpr/ppermute | solution.py:14
  423.8 6.1 %collective-permute-start.3 = (f32[128,128]{1,0:T(8,128)S(1)}, f32[128,128]{1,0:T(8,128)S(1)}, u32[]{:S(2)}, u32[]{:S(2)}) collective-permute-start(f32[128,128]{1,0:T(8,128)S(1)} %fusion.90), channel_id=1, source_target_pairs={{0,8},{8,16},{16,24},{24,32},{32,40},{40,48},{48,56},{56,64},{64,7... | collective-permute-start | bytes 196616 | tf_op jit(solution)/shard_map/while/body/eval_jaxpr/ppermute | solution.py:14
  431.5 5.9 %collective-permute-start.2 = (f32[128,128]{1,0:T(8,128)S(1)}, f32[128,128]{1,0:T(8,128)S(1)}, u32[]{:S(2)}, u32[]{:S(2)}) collective-permute-start(f32[128,128]{1,0:T(8,128)S(1)} %fusion.89), channel_id=1, source_target_pairs={{0,8},{8,16},{16,24},{24,32},{32,40},{40,48},{48,56},{56,64},{64,7... | collective-permute-start | bytes 196616 | tf_op jit(solution)/shard_map/while/body/eval_jaxpr/ppermute | solution.py:14
  431.9 6.1 %collective-permute-start.3 = (f32[128,128]{1,0:T(8,128)S(1)}, f32[128,128]{1,0:T(8,128)S(1)}, u32[]{:S(2)}, u32[]{:S(2)}) collective-permute-start(f32[128,128]{1,0:T(8,128)S(1)} %fusion.90), channel_id=1, source_target_pairs={{0,8},{8,16},{16,24},{24,32},{32,40},{40,48},{48,56},{56,64},{64,7... | collective-permute-start | bytes 196616 | tf_op jit(solution)/shard_map/while/body/eval_jaxpr/ppermute | solution.py:14
  439.7 5.9 %collective-permute-start.2 = (f32[128,128]{1,0:T(8,128)S(1)}, f32[128,128]{1,0:T(8,128)S(1)}, u32[]{:S(2)}, u32[]{:S(2)}) collective-permute-start(f32[128,128]{1,0:T(8,128)S(1)} %fusion.89), channel_id=1, source_target_pairs={{0,8},{8,16},{16,24},{24,32},{32,40},{40,48},{48,56},{56,64},{64,7... | collective-permute-start | bytes 196616 | tf_op jit(solution)/shard_map/while/body/eval_jaxpr/ppermute | solution.py:14
  440.1 6.1 %collective-permute-start.3 = (f32[128,128]{1,0:T(8,128)S(1)}, f32[128,128]{1,0:T(8,128)S(1)}, u32[]{:S(2)}, u32[]{:S(2)}) collective-permute-start(f32[128,128]{1,0:T(8,128)S(1)} %fusion.90), channel_id=1, source_target_pairs={{0,8},{8,16},{16,24},{24,32},{32,40},{40,48},{48,56},{56,64},{64,7... | collective-permute-start | bytes 196616 | tf_op jit(solution)/shard_map/while/body/eval_jaxpr/ppermute | solution.py:14
  447.9 5.9 %collective-permute-start.2 = (f32[128,128]{1,0:T(8,128)S(1)}, f32[128,128]{1,0:T(8,128)S(1)}, u32[]{:S(2)}, u32[]{:S(2)}) collective-permute-start(f32[128,128]{1,0:T(8,128)S(1)} %fusion.89), channel_id=1, source_target_pairs={{0,8},{8,16},{16,24},{24,32},{32,40},{40,48},{48,56},{56,64},{64,7... | collective-permute-start | bytes 196616 | tf_op jit(solution)/shard_map/while/body/eval_jaxpr/ppermute | solution.py:14
  448.3 6.1 %collective-permute-start.3 = (f32[128,128]{1,0:T(8,128)S(1)}, f32[128,128]{1,0:T(8,128)S(1)}, u32[]{:S(2)}, u32[]{:S(2)}) collective-permute-start(f32[128,128]{1,0:T(8,128)S(1)} %fusion.90), channel_id=1, source_target_pairs={{0,8},{8,16},{16,24},{24,32},{32,40},{40,48},{48,56},{56,64},{64,7... | collective-permute-start | bytes 196616 | tf_op jit(solution)/shard_map/while/body/eval_jaxpr/ppermute | solution.py:14
  456.5 6.1 %collective-permute-start.3 = (f32[128,128]{1,0:T(8,128)S(1)}, f32[128,128]{1,0:T(8,128)S(1)}, u32[]{:S(2)}, u32[]{:S(2)}) collective-permute-start(f32[128,128]{1,0:T(8,128)S(1)} %fusion.90), channel_id=1, source_target_pairs={{0,8},{8,16},{16,24},{24,32},{32,40},{40,48},{48,56},{56,64},{64,7... | collective-permute-start | bytes 196616 | tf_op jit(solution)/shard_map/while/body/eval_jaxpr/ppermute | solution.py:14
  464.2 5.9 %collective-permute-start.2 = (f32[128,128]{1,0:T(8,128)S(1)}, f32[128,128]{1,0:T(8,128)S(1)}, u32[]{:S(2)}, u32[]{:S(2)}) collective-permute-start(f32[128,128]{1,0:T(8,128)S(1)} %fusion.89), channel_id=1, source_target_pairs={{0,8},{8,16},{16,24},{24,32},{32,40},{40,48},{48,56},{56,64},{64,7... | collective-permute-start | bytes 196616 | tf_op jit(solution)/shard_map/while/body/eval_jaxpr/ppermute | solution.py:14
  464.6 6.1 %collective-permute-start.3 = (f32[128,128]{1,0:T(8,128)S(1)}, f32[128,128]{1,0:T(8,128)S(1)}, u32[]{:S(2)}, u32[]{:S(2)}) collective-permute-start(f32[128,128]{1,0:T(8,128)S(1)} %fusion.90), channel_id=1, source_target_pairs={{0,8},{8,16},{16,24},{24,32},{32,40},{40,48},{48,56},{56,64},{64,7... | collective-permute-start | bytes 196616 | tf_op jit(solution)/shard_map/while/body/eval_jaxpr/ppermute | solution.py:14
  472.8 6.1 %collective-permute-start.3 = (f32[128,128]{1,0:T(8,128)S(1)}, f32[128,128]{1,0:T(8,128)S(1)}, u32[]{:S(2)}, u32[]{:S(2)}) collective-permute-start(f32[128,128]{1,0:T(8,128)S(1)} %fusion.90), channel_id=1, source_target_pairs={{0,8},{8,16},{16,24},{24,32},{32,40},{40,48},{48,56},{56,64},{64,7... | collective-permute-start | bytes 196616 | tf_op jit(solution)/shard_map/while/body/eval_jaxpr/ppermute | solution.py:14
  481.0 6.1 %collective-permute-start.3 = (f32[128,128]{1,0:T(8,128)S(1)}, f32[128,128]{1,0:T(8,128)S(1)}, u32[]{:S(2)}, u32[]{:S(2)}) collective-permute-start(f32[128,128]{1,0:T(8,128)S(1)} %fusion.90), channel_id=1, source_target_pairs={{0,8},{8,16},{16,24},{24,32},{32,40},{40,48},{48,56},{56,64},{64,7... | collective-permute-start | bytes 196616 | tf_op jit(solution)/shard_map/while/body/eval_jaxpr/ppermute | solution.py:14
  488.7 5.9 %collective-permute-start.2 = (f32[128,128]{1,0:T(8,128)S(1)}, f32[128,128]{1,0:T(8,128)S(1)}, u32[]{:S(2)}, u32[]{:S(2)}) collective-permute-start(f32[128,128]{1,0:T(8,128)S(1)} %fusion.89), channel_id=1, source_target_pairs={{0,8},{8,16},{16,24},{24,32},{32,40},{40,48},{48,56},{56,64},{64,7... | collective-permute-start | bytes 196616 | tf_op jit(solution)/shard_map/while/body/eval_jaxpr/ppermute | solution.py:14
  489.2 6.1 %collective-permute-start.3 = (f32[128,128]{1,0:T(8,128)S(1)}, f32[128,128]{1,0:T(8,128)S(1)}, u32[]{:S(2)}, u32[]{:S(2)}) collective-permute-start(f32[128,128]{1,0:T(8,128)S(1)} %fusion.90), channel_id=1, source_target_pairs={{0,8},{8,16},{16,24},{24,32},{32,40},{40,48},{48,56},{56,64},{64,7... | collective-permute-start | bytes 196616 | tf_op jit(solution)/shard_map/while/body/eval_jaxpr/ppermute | solution.py:14
  497.4 6.1 %collective-permute-start.3 = (f32[128,128]{1,0:T(8,128)S(1)}, f32[128,128]{1,0:T(8,128)S(1)}, u32[]{:S(2)}, u32[]{:S(2)}) collective-permute-start(f32[128,128]{1,0:T(8,128)S(1)} %fusion.90), channel_id=1, source_target_pairs={{0,8},{8,16},{16,24},{24,32},{32,40},{40,48},{48,56},{56,64},{64,7... | collective-permute-start | bytes 196616 | tf_op jit(solution)/shard_map/while/body/eval_jaxpr/ppermute | solution.py:14
  505.1 5.9 %collective-permute-start.2 = (f32[128,128]{1,0:T(8,128)S(1)}, f32[128,128]{1,0:T(8,128)S(1)}, u32[]{:S(2)}, u32[]{:S(2)}) collective-permute-start(f32[128,128]{1,0:T(8,128)S(1)} %fusion.89), channel_id=1, source_target_pairs={{0,8},{8,16},{16,24},{24,32},{32,40},{40,48},{48,56},{56,64},{64,7... | collective-permute-start | bytes 196616 | tf_op jit(solution)/shard_map/while/body/eval_jaxpr/ppermute | solution.py:14
  505.5 6.1 %collective-permute-start.3 = (f32[128,128]{1,0:T(8,128)S(1)}, f32[128,128]{1,0:T(8,128)S(1)}, u32[]{:S(2)}, u32[]{:S(2)}) collective-permute-start(f32[128,128]{1,0:T(8,128)S(1)} %fusion.90), channel_id=1, source_target_pairs={{0,8},{8,16},{16,24},{24,32},{32,40},{40,48},{48,56},{56,64},{64,7... | collective-permute-start | bytes 196616 | tf_op jit(solution)/shard_map/while/body/eval_jaxpr/ppermute | solution.py:14
  513.3 5.9 %collective-permute-start.2 = (f32[128,128]{1,0:T(8,128)S(1)}, f32[128,128]{1,0:T(8,128)S(1)}, u32[]{:S(2)}, u32[]{:S(2)}) collective-permute-start(f32[128,128]{1,0:T(8,128)S(1)} %fusion.89), channel_id=1, source_target_pairs={{0,8},{8,16},{16,24},{24,32},{32,40},{40,48},{48,56},{56,64},{64,7... | collective-permute-start | bytes 196616 | tf_op jit(solution)/shard_map/while/body/eval_jaxpr/ppermute | solution.py:14
  513.7 6.1 %collective-permute-start.3 = (f32[128,128]{1,0:T(8,128)S(1)}, f32[128,128]{1,0:T(8,128)S(1)}, u32[]{:S(2)}, u32[]{:S(2)}) collective-permute-start(f32[128,128]{1,0:T(8,128)S(1)} %fusion.90), channel_id=1, source_target_pairs={{0,8},{8,16},{16,24},{24,32},{32,40},{40,48},{48,56},{56,64},{64,7... | collective-permute-start | bytes 196616 | tf_op jit(solution)/shard_map/while/body/eval_jaxpr/ppermute | solution.py:14
  521.4 5.9 %collective-permute-start.2 = (f32[128,128]{1,0:T(8,128)S(1)}, f32[128,128]{1,0:T(8,128)S(1)}, u32[]{:S(2)}, u32[]{:S(2)}) collective-permute-start(f32[128,128]{1,0:T(8,128)S(1)} %fusion.89), channel_id=1, source_target_pairs={{0,8},{8,16},{16,24},{24,32},{32,40},{40,48},{48,56},{56,64},{64,7... | collective-permute-start | bytes 196616 | tf_op jit(solution)/shard_map/while/body/eval_jaxpr/ppermute | solution.py:14
  521.9 6.1 %collective-permute-start.3 = (f32[128,128]{1,0:T(8,128)S(1)}, f32[128,128]{1,0:T(8,128)S(1)}, u32[]{:S(2)}, u32[]{:S(2)}) collective-permute-start(f32[128,128]{1,0:T(8,128)S(1)} %fusion.90), channel_id=1, source_target_pairs={{0,8},{8,16},{16,24},{24,32},{32,40},{40,48},{48,56},{56,64},{64,7... | collective-permute-start | bytes 196616 | tf_op jit(solution)/shard_map/while/body/eval_jaxpr/ppermute | solution.py:14
  529.6 5.9 %collective-permute-start.2 = (f32[128,128]{1,0:T(8,128)S(1)}, f32[128,128]{1,0:T(8,128)S(1)}, u32[]{:S(2)}, u32[]{:S(2)}) collective-permute-start(f32[128,128]{1,0:T(8,128)S(1)} %fusion.89), channel_id=1, source_target_pairs={{0,8},{8,16},{16,24},{24,32},{32,40},{40,48},{48,56},{56,64},{64,7... | collective-permute-start | bytes 196616 | tf_op jit(solution)/shard_map/while/body/eval_jaxpr/ppermute | solution.py:14
  530.1 6.1 %collective-permute-start.3 = (f32[128,128]{1,0:T(8,128)S(1)}, f32[128,128]{1,0:T(8,128)S(1)}, u32[]{:S(2)}, u32[]{:S(2)}) collective-permute-start(f32[128,128]{1,0:T(8,128)S(1)} %fusion.90), channel_id=1, source_target_pairs={{0,8},{8,16},{16,24},{24,32},{32,40},{40,48},{48,56},{56,64},{64,7... | collective-permute-start | bytes 196616 | tf_op jit(solution)/shard_map/while/body/eval_jaxpr/ppermute | solution.py:14
  (70 other events, 450.9 us)
Sparse Core Ops, SparseCore 0:
  10.6 64.6 all-gather.3
  77.0 121.9 all-gather.5
  201.4 62.7 all-gather.7
